TPU v7x, 128 devices: a whole 4x4x4 slice. The times are simulated.
128 devices in a mesh: expert: 8 (over y, z_lo), fsdp: 16 (over x, z_hi, core).
Axes of the slice: x: 4, y: 4, z: 4 (z_hi: 2, z_lo: 2; z = z_hi * 2 + z_lo), core: 2. Of those that a mesh axis runs over, the one named last changes fastest.
Arguments:
- tokens: bfloat16 [18432, 2048], P(('expert', 'fsdp')), may hold values from -6 to 6
- expert_ids: int32 [18432, 6], P(('expert', 'fsdp')), may hold values from 0 to 15, as said below
- combine: float32 [18432, 6], P(('expert', 'fsdp')), may hold values from 0.05 to 1
- gate_weight: bfloat16 [16, 1408, 2048], P('expert', 'fsdp'), may hold values from -0.125 to 0.125
- up_weight: bfloat16 [16, 1408, 2048], P('expert', 'fsdp'), may hold values from -0.125 to 0.125
- down_weight: bfloat16 [16, 1408, 2048], P('expert', 'fsdp'), may hold values from -0.15625 to 0.15625
Outputs:
- mixed: bfloat16 [18432, 2048], P(('expert', 'fsdp'))
Inputs may be any that keep to these rules, and one draw needn't show every extreme that they name: `expert_ids`: each row names 6 different experts. Within the 144 rows of each device no expert is named more than 72 times, and one and the same expert is named exactly 72 times by the rows of every device.
All inputs are finite; a program needn't handle non-finite values.
Results may differ from a plain program's by a relative error of at most 0.0058.
Values may be sent and summed in bfloat16 or wider, within the bound.
A program may use at most 128 MiB of HBM per device.

v0:
```python
import jax
import jax.numpy as jnp
from jax import lax
from jax.sharding import PartitionSpec as P

CAP = 72


def add_piece(expert_rows, pieces):
    gate_piece, up_piece, down_piece = pieces
    gate_pre = jnp.einsum(
        "grd,gfd->grf", expert_rows, gate_piece, preferred_element_type=jnp.float32
    )
    up_pre = jnp.einsum("grd,gfd->grf", expert_rows, up_piece, preferred_element_type=jnp.float32)
    hidden = (jax.nn.silu(gate_pre) * up_pre).astype(jnp.bfloat16)
    return jnp.einsum("grf,gfd->grd", hidden, down_piece, preferred_element_type=jnp.float32)


def per_device(tokens, expert_ids, combine, gate_weight, up_weight, down_weight):
    groups = lax.axis_size("expert")
    per_group = gate_weight.shape[0]
    tok_rows, top_k = expert_ids.shape
    model_width = tokens.shape[1]
    flat_ids = expert_ids.reshape(-1)
    onehot = (flat_ids[:, None] == jnp.arange(per_group * groups, dtype=jnp.int32)[None, :]).astype(
        jnp.int32
    )
    earlier = jnp.cumsum(onehot, axis=0) - onehot
    rank_within = jnp.sum(earlier * onehot, axis=1)
    owner_group = flat_ids // per_group
    within = flat_ids % per_group
    slot_index = (within * groups + owner_group) * CAP + rank_within
    source = jnp.arange(tok_rows * top_k, dtype=jnp.int32) // top_k
    outgoing = (
        jnp.zeros((per_group * groups * CAP, model_width), jnp.bfloat16)
        .at[slot_index]
        .set(tokens[source])
    )
    outgoing = outgoing.reshape(per_group, groups, CAP, model_width)
    arrived = lax.all_to_all(outgoing, "expert", split_axis=1, concat_axis=1, tiled=True)
    expert_rows = arrived.reshape(per_group, groups * CAP, model_width)
    summed = add_piece(
        expert_rows,
        (
            lax.all_gather(gate_weight, "fsdp", axis=1, tiled=True),
            lax.all_gather(up_weight, "fsdp", axis=1, tiled=True),
            lax.all_gather(down_weight, "fsdp", axis=1, tiled=True),
        ),
    )
    produced = summed.astype(jnp.bfloat16)
    produced = produced.reshape(per_group, groups, CAP, model_width)
    returned = lax.all_to_all(produced, "expert", split_axis=1, concat_axis=1, tiled=True)
    back_rows = returned.reshape(per_group * groups * CAP, model_width)[slot_index]
    weighted = (
        back_rows.astype(jnp.float32).reshape(tok_rows, top_k, model_width) * combine[:, :, None]
    )
    return jnp.sum(weighted, axis=1).astype(jnp.bfloat16)


def solution(mesh):
    return jax.shard_map(
        per_device,
        mesh=mesh,
        in_specs=(
            P(("expert", "fsdp"), None),
            P(("expert", "fsdp"), None),
            P(("expert", "fsdp"), None),
            P("expert", "fsdp", None),
            P("expert", "fsdp", None),
            P("expert", "fsdp", None),
        ),
        out_specs=P(("expert", "fsdp"), None),
        check_vma=False,
    )
```

profile of v0, /device:TPU:1, one launch (start us, length us, event | category | flops | bytes accessed | tf_op | source)
XLA Modules:
  0.0 457.1 jit_solution(14942654767058175792)
XLA Ops:
  6.5 0.0 copy-start
  6.5 0.0 all-gather.4.cloned.1.call-start
  6.5 0.7 all-gather.4.cloned.1.call-update
  7.3 0.0 all-gather.6.cloned.1.call-start
  7.3 0.7 all-gather.6.cloned.1.call-update
  8.0 0.0 all-gather.8.cloned.1.call-start
  8.1 0.7 all-gather.8.cloned.1.call-update
  8.7 0.8 copy.21
  9.5 0.1 eq.24
  9.7 0.1 reshape.195
  9.9 2.0 reduce-window.6
  11.9 0.3 slice_reduce_fusion
  12.2 0.1 bitcast_bitcast_fusion
  12.4 0.0 copy-done
  12.4 23.2 %scatter_custom_fusion = bf16[1152,2048]{1,0:T(8,128)(2,1)} fusion(s32[864]{0:T(1024)S(1)} %fusion.5, bf16[144,2048]{1,0:T(8,128)(2,1)S(1)} %copy-done, s32[1024]{0:T(1024)S(1)} %pad_clamp_fusion.1, bf16[]{:T(256)} %constant.42.clone.1), kind=kCustom, calls=%fused_computation.6 | custom fusion | bytes 4718594 | tf_op jit(solution)/shard_map/scatter | solution.py:37
  35.6 2.8 copy.25
  38.4 66.5 %all_to_all.10 = bf16[2,8,72,2048]{3,2,0,1:T(8,128)(2,1)S(1)} all-to-all(bf16[2,8,72,2048]{3,2,0,1:T(8,128)(2,1)S(1)} %copy.25), channel_id=1, replica_groups=mesh['expert'=8,'fsdp'=16] {'expert'}, dimensions={1} | all-to-all | bytes 9437184 | tf_op jit(solution)/shard_map/all_to_all | solution.py:40
  104.9 2.5 copy.26
  107.4 38.9 %all-gather.4.cloned.1.call-done = bf16[2,1408,2048]{2,1,0:T(8,128)(2,1)} async-done(((bf16[2,88,2048]{2,1,0:T(8,128)(2,1)}), bf16[2,1408,2048]{2,1,0:T(8,128)(2,1)}) %all-gather.4.cloned.1.call-update) | async-done | bytes 11534352 | tf_op jit(solution)/shard_map/all_gather | solution.py:45
  146.3 14.4 %fusion.9 = f32[2,576,1408]{2,1,0:T(8,128)} fusion(bf16[2,576,2048]{2,1,0:T(8,128)(2,1)} %bitcast.33, bf16[2,1408,2048]{2,1,0:T(8,128)(2,1)} %all-gather.4.cloned.1.call-done), kind=kOutput, calls=%fused_computation.36 | convolution fusion | flops 6643777536 | bytes 22740992 | tf_op jit(solution)/shard_map/grd,gfd->grf/dot_general | solution.py:11
  160.7 71.9 %all-gather.6.cloned.1.call-done = bf16[2,1408,2048]{2,1,0:T(8,128)(2,1)} async-done(((bf16[2,88,2048]{2,1,0:T(8,128)(2,1)}), bf16[2,1408,2048]{2,1,0:T(8,128)(2,1)}) %all-gather.6.cloned.1.call-update) | async-done | bytes 11534352 | tf_op jit(solution)/shard_map/all_gather | solution.py:46
  232.6 86.3 %all-gather.8.cloned.1.call-done = bf16[2,1408,2048]{2,1,0:T(8,128)(2,1)} async-done(((bf16[2,88,2048]{2,1,0:T(8,128)(2,1)}), bf16[2,1408,2048]{2,1,0:T(8,128)(2,1)}) %all-gather.8.cloned.1.call-update) | async-done | bytes 11534352 | tf_op jit(solution)/shard_map/all_gather | solution.py:47
  318.8 22.8 %convolution_convert_fusion = bf16[2,576,2048]{2,1,0:T(8,128)(2,1)} fusion(bf16[2,1408,2048]{2,1,0:T(8,128)(2,1)} %all-gather.8.cloned.1.call-done, f32[2,576,1408]{2,1,0:T(8,128)} %fusion.9, bf16[2,576,2048]{2,1,0:T(8,128)(2,1)} %bitcast.34, bf16[2,1408,2048]{2,1,0:T(8,128)(2,1)} %all-gather.6.cloned.1.call-done), kind=kOutput, calls=%fused_computation.5 | convolution fusion | flops 13299646464 | bytes 38993920 | tf_op jit(solution)/shard_map/grf,gfd->grd/dot_general | solution.py:16
  341.6 5.2 %copy.27 = bf16[2,8,72,2048]{3,2,0,1:T(8,128)(2,1)} copy(bf16[2,8,72,2048]{3,2,1,0:T(8,128)(2,1)} %bitcast.35) | data formatting | bytes 9437184 | tf_op jit(solution)/shard_map/reshape | solution.py:51
  346.9 4.9 %all-to-all-start.1 = ((bf16[2,8,72,2048]{3,2,0,1:T(8,128)(2,1)}), bf16[2,8,72,2048]{3,2,0,1:T(8,128)(2,1)}, u32[]{:S(2)}, u32[]{:S(2)}) async-start(bf16[2,8,72,2048]{3,2,0,1:T(8,128)(2,1)} %copy.27), calls=%async_computation.1 | async-start | bytes 9437184 | tf_op jit(solution)/shard_map/all_to_all | solution.py:52
  351.8 0.0 copy-done.2
  351.8 0.1 copy.29
  351.9 66.3 %all-to-all-done.1 = bf16[2,8,72,2048]{3,2,0,1:T(8,128)(2,1)} async-done(((bf16[2,8,72,2048]{3,2,0,1:T(8,128)(2,1)}), bf16[2,8,72,2048]{3,2,0,1:T(8,128)(2,1)}, u32[]{:S(2)}, u32[]{:S(2)}) %all-to-all-start.1) | async-done | bytes 4718624 | tf_op jit(solution)/shard_map/all_to_all | solution.py:52
  418.2 5.2 %copy.28 = bf16[2,8,72,2048]{3,2,1,0:T(8,128)(2,1)} copy(bf16[2,8,72,2048]{3,2,0,1:T(8,128)(2,1)} %all-to-all-done.1) | data formatting | bytes 9437184 | tf_op jit(solution)/shard_map/all_to_all | solution.py:52
  423.5 11.7 %gather_fusion = bf16[864,2048]{1,0:T(8,128)(2,1)} fusion(bf16[1152,2048]{1,0:T(8,128)(2,1)} %bitcast.31, s32[1024]{0:T(1024)S(1)} %pad_clamp_fusion), kind=kCustom, calls=%fused_computation.1 | custom fusion | bytes 7081344 | tf_op jit(solution)/shard_map/gather | solution.py:53
  435.2 7.2 %reshape.203 = f32[144,6,2048]{2,1,0:T(8,128)} reshape(bf16[864,2048]{1,0:T(8,128)(2,1)} %gather_fusion) | data formatting | bytes 10616832 | tf_op jit(solution)/shard_map/convert_element_type | solution.py:55
  442.4 8.2 %multiply_reduce_fusion = bf16[144,2048]{1,0:T(8,128)(2,1)} fusion(f32[144,6,2048]{2,1,0:T(8,128)} %reshape.203, f32[144,6]{1,0:T(8,128)S(1)} %copy.29), kind=kLoop, calls=%fused_computation.3 | loop fusion | flops 3244032 | bytes 7671168 | tf_op jit(solution)/shard_map/reduce_sum | solution.py:57
  (11 shorter events, 0.2 us)
Async XLA Ops:
  6.5 5.9 %copy-start = (bf16[144,2048]{1,0:T(8,128)(2,1)S(1)}, bf16[144,2048]{1,0:T(8,128)(2,1)}, u32[]{:S(2)}) copy-start(bf16[144,2048]{1,0:T(8,128)(2,1)} %param.6) | copy-start | bytes 1769476
  6.5 139.8 %all-gather.4.cloned.1.call-start = ((), (), s32[]{:S(2)}) async-start(), calls=%async_computation.2 | async-start | bytes 12255232 | tf_op jit(solution)/shard_map/all_gather | solution.py:45
  7.3 225.3 %all-gather.6.cloned.1.call-start = ((), (), s32[]{:S(2)}) async-start(), calls=%async_computation.3 | async-start | bytes 12255232 | tf_op jit(solution)/shard_map/all_gather | solution.py:46
  8.0 310.8 %all-gather.8.cloned.1.call-start = ((), (), s32[]{:S(2)}) async-start(), calls=%async_computation.4 | async-start | bytes 12255232 | tf_op jit(solution)/shard_map/all_gather | solution.py:47
  346.9 5.0 %copy-start.2 = (f32[144,6]{0,1:T(8,128)S(1)}, f32[144,6]{0,1:T(8,128)}, u32[]{:S(2)}) copy-start(f32[144,6]{0,1:T(8,128)} %param.8) | copy-start | bytes 10372
  346.9 71.4 %all-to-all-start.1 = ((bf16[2,8,72,2048]{3,2,0,1:T(8,128)(2,1)}), bf16[2,8,72,2048]{3,2,0,1:T(8,128)(2,1)}, u32[]{:S(2)}, u32[]{:S(2)}) async-start(bf16[2,8,72,2048]{3,2,0,1:T(8,128)(2,1)} %copy.27), calls=%async_computation.1 | async-start | bytes 9437184 | tf_op jit(solution)/shard_map/all_to_all | solution.py:52
  435.2 15.4 %copy-start.1 = (bf16[144,2048]{1,0:T(8,128)(2,1)S(1)}, bf16[144,2048]{1,0:T(8,128)(2,1)}, u32[]{:S(2)}) copy-start(bf16[144,2048]{1,0:T(8,128)(2,1)} %param.6) | copy-start | bytes 1769476
Sparse Core Ops, SparseCore 0:
  9.8 136.4 all-gather.3
  148.8 83.7 all-gather.5
  235.1 83.7 all-gather.7
where the time goes:
time: 458 us; the launch traced here: 457 us
  waiting for transfers between devices  265 us (58%)
  blocking collectives  66.5 us (15%)
  local copies, waits for them, and re-layouts  59.3 us (13%)
  matrix products  37.2 us (8%)
  between operations  13.2 us (3%)
  other arithmetic  10.4 us (2%)
  starting transfers between devices  5.02 us (1%)
    all_gather x1, waiting for transfers between devices, per_device(): lax.all_gather(down_weight, 'fsdp', axis=1, tiled=True)  86.3 us
    all_gather x1, waiting for transfers between devices, per_device(): lax.all_gather(up_weight, 'fsdp', axis=1, tiled=True)  71.9 us
    all_to_all x1, blocking collectives, per_device(): lax.all_to_all(outgoing, 'expert', split_axis=1, concat_axis=1, tiled=True)  66.5 us
    all_to_all x1, waiting for transfers between devices, per_device(): lax.all_to_all(produced, 'expert', split_axis=1, concat_axis=1, tiled=True)  66.3 us
    all_gather x1, waiting for transfers between devices, per_device(): lax.all_gather(gate_weight, 'fsdp', axis=1, tiled=True)  38.9 us
    scatter x1, local copies, waits for them, and re-layouts, per_device(): outgoing = jnp.zeros((per_group * groups * CAP, model_width), jnp.bfloat1...  23.2 us
    dot_general x1, matrix products, add_piece(): jnp.einsum('grf,gfd->grd', hidden, down_piece, preferred_element_type=jnp...  22.8 us
    dot_general x1, matrix products, add_piece(): jnp.einsum('grd,gfd->grf', expert_rows, gate_piece, preferred_element_typ...  14.4 us
  transfers between devices with their start and end apart: 4, of which 4 were waited for; matrix products, arithmetic and copies ran while one was open for 10% of the time, Pallas kernels for 0%

commit v1 on v0

--- a/solution.py
+++ b/solution.py
@@ -4,6 +4,13 @@
 from jax.sharding import PartitionSpec as P
 
 CAP = 72
+
+
+def trade_parts(x, axis, split, join):
+    size = lax.axis_size(axis)
+    blocks = jnp.stack(jnp.split(x, size, axis=split), axis=0)
+    blocks = lax.all_to_all(blocks, axis, split_axis=0, concat_axis=0)
+    return jnp.concatenate(blocks, axis=join)
 
 
 def add_piece(expert_rows, pieces):
@@ -49,7 +56,7 @@
     )
     produced = summed.astype(jnp.bfloat16)
     produced = produced.reshape(per_group, groups, CAP, model_width)
-    returned = lax.all_to_all(produced, "expert", split_axis=1, concat_axis=1, tiled=True)
+    returned = trade_parts(produced, "expert", 1, 1)
     back_rows = returned.reshape(per_group * groups * CAP, model_width)[slot_index]
     weighted = (
         back_rows.astype(jnp.float32).reshape(tok_rows, top_k, model_width) * combine[:, :, None]

time: 458 us -> 464 us (1.013)
  local copies, waits for them, and re-layouts: 59.3 us -> 65.6 us
    unnamed x8 -> x17, local copies, waits for them, and re-layouts: 0.91 us -> 11.5 us
    all_to_all x1 -> x0, local copies, waits for them, and re-layouts: 5.23 us -> none  [per_device(): lax.all_to_all(produced, 'expert', split_axis=1, concat_axis=1, tiled=True)]
where the time goes in v1:
time: 464 us; the launch traced here: 463 us
  waiting for transfers between devices  265 us (57%)
  blocking collectives  66.5 us (14%)
  local copies, waits for them, and re-layouts  65.6 us (14%)
  matrix products  37.2 us (8%)
  between operations  13.2 us (3%)
  other arithmetic  10.4 us (2%)
  starting transfers between devices  5.02 us (1%)
    all_gather x1, waiting for transfers between devices, per_device(): lax.all_gather(down_weight, 'fsdp', axis=1, tiled=True)  86.3 us
    all_gather x1, waiting for transfers between devices, per_device(): lax.all_gather(up_weight, 'fsdp', axis=1, tiled=True)  71.9 us
    all_to_all x1, blocking collectives, per_device(): lax.all_to_all(outgoing, 'expert', split_axis=1, concat_axis=1, tiled=True)  66.5 us
    all_to_all x1, waiting for transfers between devices, trade_parts(): blocks = lax.all_to_all(blocks, axis, split_axis=0, concat_axis=0)  66.3 us
    all_gather x1, waiting for transfers between devices, per_device(): lax.all_gather(gate_weight, 'fsdp', axis=1, tiled=True)  38.9 us
    scatter x1, local copies, waits for them, and re-layouts, per_device(): outgoing = jnp.zeros((per_group * groups * CAP, model_width), jnp.bfloat1...  23.2 us
    dot_general x1, matrix products, add_piece(): jnp.einsum('grf,gfd->grd', hidden, down_piece, preferred_element_type=jnp...  22.8 us
    dot_general x1, matrix products, add_piece(): jnp.einsum('grd,gfd->grf', expert_rows, gate_piece, preferred_element_typ...  14.4 us
  transfers between devices with their start and end apart: 4, of which 4 were waited for; matrix products, arithmetic and copies ran while one was open for 10% of the time, Pallas kernels for 0%

profile of v1, /device:TPU:1, one launch (start us, length us, event | category | flops | bytes accessed | tf_op | source)
XLA Modules:
  0.0 463.4 jit_solution(16629838561561609754)
XLA Ops:
  6.5 0.7 all-gather.4.cloned.1.call-update
  7.3 0.7 all-gather.6.cloned.1.call-update
  8.1 0.7 all-gather.8.cloned.1.call-update
  8.7 0.8 copy.43
  9.5 0.1 eq.24
  9.7 0.1 reshape.195
  9.9 2.0 reduce-window.6
  11.9 0.3 slice_reduce_fusion
  12.4 23.2 %scatter_custom_fusion = bf16[1152,2048]{1,0:T(8,128)(2,1)} fusion(s32[864]{0:T(1024)S(1)} %fusion.13, bf16[144,2048]{1,0:T(8,128)(2,1)S(1)} %copy-done, s32[1024]{0:T(1024)S(1)} %get-tuple-element.6, bf16[]{:T(256)} %constant.42.clone.1), kind=kCustom, calls=%fused_computation.6 | custom fusion | bytes 4718594 | tf_op jit(solution)/shard_map/scatter | solution.py:44
  35.6 2.8 copy.47
  38.4 66.5 %all_to_all.10 = bf16[2,8,72,2048]{3,2,0,1:T(8,128)(2,1)S(1)} all-to-all(bf16[2,8,72,2048]{3,2,0,1:T(8,128)(2,1)S(1)} %copy.47), channel_id=1, replica_groups=mesh['expert'=8,'fsdp'=16] {'expert'}, dimensions={1} | all-to-all | bytes 9437184 | tf_op jit(solution)/shard_map/all_to_all | solution.py:47
  104.9 2.5 copy.48
  107.4 38.9 %all-gather.4.cloned.1.call-done = bf16[2,1408,2048]{2,1,0:T(8,128)(2,1)} async-done(((bf16[2,88,2048]{2,1,0:T(8,128)(2,1)}), bf16[2,1408,2048]{2,1,0:T(8,128)(2,1)}) %all-gather.4.cloned.1.call-update) | async-done | bytes 11534352 | tf_op jit(solution)/shard_map/all_gather | solution.py:52
  146.3 14.4 %fusion.17 = f32[2,576,1408]{2,1,0:T(8,128)} fusion(bf16[2,576,2048]{2,1,0:T(8,128)(2,1)} %bitcast.80, bf16[2,1408,2048]{2,1,0:T(8,128)(2,1)} %all-gather.4.cloned.1.call-done), kind=kOutput, calls=%fused_computation.52 | convolution fusion | flops 6643777536 | bytes 22740992 | tf_op jit(solution)/shard_map/grd,gfd->grf/dot_general | solution.py:18
  160.7 71.9 %all-gather.6.cloned.1.call-done = bf16[2,1408,2048]{2,1,0:T(8,128)(2,1)} async-done(((bf16[2,88,2048]{2,1,0:T(8,128)(2,1)}), bf16[2,1408,2048]{2,1,0:T(8,128)(2,1)}) %all-gather.6.cloned.1.call-update) | async-done | bytes 11534352 | tf_op jit(solution)/shard_map/all_gather | solution.py:53
  232.6 86.3 %all-gather.8.cloned.1.call-done = bf16[2,1408,2048]{2,1,0:T(8,128)(2,1)} async-done(((bf16[2,88,2048]{2,1,0:T(8,128)(2,1)}), bf16[2,1408,2048]{2,1,0:T(8,128)(2,1)}) %all-gather.8.cloned.1.call-update) | async-done | bytes 11534352 | tf_op jit(solution)/shard_map/all_gather | solution.py:54
  318.8 22.8 %convolution_convert_fusion = bf16[2,576,2048]{2,1,0:T(8,128)(2,1)} fusion(bf16[2,1408,2048]{2,1,0:T(8,128)(2,1)} %all-gather.8.cloned.1.call-done, f32[2,576,1408]{2,1,0:T(8,128)} %fusion.17, bf16[2,576,2048]{2,1,0:T(8,128)(2,1)} %bitcast.81, bf16[2,1408,2048]{2,1,0:T(8,128)(2,1)} %all-gather.6.cloned.1.call-done), kind=kOutput, calls=%fused_computation.5 | convolution fusion | flops 13299646464 | bytes 38993920 | tf_op jit(solution)/shard_map/grf,gfd->grd/dot_general | solution.py:23
  341.6 2.1 fusion.10
  343.7 1.9 fusion.9
  345.7 1.9 fusion.8
  347.6 1.9 fusion.7
  349.6 0.9 fusion.6
  350.4 0.9 fusion.5
  351.3 0.9 fusion.4
  352.2 1.0 fusion.3
  353.2 4.9 %all-to-all-start.1 = ((bf16[8,2,1,72,2048]{4,3,1,2,0:T(8,128)(2,1)}), bf16[8,2,1,72,2048]{4,3,1,2,0:T(8,128)(2,1)}, u32[]{:S(2)}, u32[]{:S(2)}) async-start(bf16[8,2,1,72,2048]{4,3,1,2,0:T(8,128)(2,1)} %fusion.3), calls=%async_computation.1 | async-start | bytes 9437184 | tf_op jit(solution)/shard_map/all_to_all | solution.py:12
  358.1 0.1 copy.57
  358.3 66.3 %all-to-all-done.1 = bf16[8,2,1,72,2048]{4,3,1,2,0:T(8,128)(2,1)} async-done(((bf16[8,2,1,72,2048]{4,3,1,2,0:T(8,128)(2,1)}), bf16[8,2,1,72,2048]{4,3,1,2,0:T(8,128)(2,1)}, u32[]{:S(2)}, u32[]{:S(2)}) %all-to-all-start.1) | async-done | bytes 4718624 | tf_op jit(solution)/shard_map/all_to_all | solution.py:12
  424.6 5.2 %copy.56 = bf16[2,8,1,72,2048]{4,3,1,0,2:T(8,128)(2,1)} copy(bf16[2,8,1,72,2048]{4,3,0,2,1:T(8,128)(2,1)} %bitcast.12) | data formatting | bytes 9437184 | tf_op jit(solution)/shard_map/reshape | solution.py:13
  429.8 11.7 %gather_fusion = bf16[864,2048]{1,0:T(8,128)(2,1)} fusion(bf16[1152,2048]{1,0:T(8,128)(2,1)} %bitcast.78, s32[1024]{0:T(1024)S(1)} %get-tuple-element.5), kind=kCustom, calls=%fused_computation.1 | custom fusion | bytes 7081344 | tf_op jit(solution)/shard_map/gather | solution.py:60
  441.5 7.2 %reshape.203 = f32[144,6,2048]{2,1,0:T(8,128)} reshape(bf16[864,2048]{1,0:T(8,128)(2,1)} %gather_fusion) | data formatting | bytes 10616832 | tf_op jit(solution)/shard_map/convert_element_type | solution.py:62
  448.7 8.2 %multiply_reduce_fusion = bf16[144,2048]{1,0:T(8,128)(2,1)} fusion(f32[144,6,2048]{2,1,0:T(8,128)} %reshape.203, f32[144,6]{1,0:T(8,128)S(1)} %copy.57), kind=kLoop, calls=%fused_computation.3 | loop fusion | flops 3244032 | bytes 7671168 | tf_op jit(solution)/shard_map/reduce_sum | solution.py:64
  (19 shorter events, 0.3 us)
Async XLA Ops:
  6.5 5.9 %copy-start = (bf16[144,2048]{1,0:T(8,128)(2,1)S(1)}, bf16[144,2048]{1,0:T(8,128)(2,1)}, u32[]{:S(2)}) copy-start(bf16[144,2048]{1,0:T(8,128)(2,1)} %param.6) | copy-start | bytes 1769476
  6.5 139.8 %all-gather.4.cloned.1.call-start = ((), (), s32[]{:S(2)}) async-start(), calls=%async_computation.2 | async-start | bytes 12255232 | tf_op jit(solution)/shard_map/all_gather | solution.py:52
  7.3 225.3 %all-gather.6.cloned.1.call-start = ((), (), s32[]{:S(2)}) async-start(), calls=%async_computation.3 | async-start | bytes 12255232 | tf_op jit(solution)/shard_map/all_gather | solution.py:53
  8.0 310.8 %all-gather.8.cloned.1.call-start = ((), (), s32[]{:S(2)}) async-start(), calls=%async_computation.4 | async-start | bytes 12255232 | tf_op jit(solution)/shard_map/all_gather | solution.py:54
  341.6 7.9 %copy-start.2 = (bf16[2,576,2048]{2,1,0:T(8,128)(2,1)S(1)}, bf16[2,576,2048]{2,1,0:T(8,128)(2,1)}, u32[]{:S(2)}) copy-start(bf16[2,576,2048]{2,1,0:T(8,128)(2,1)} %convolution_convert_fusion) | copy-start | bytes 14155780
  353.2 5.0 %copy-start.3 = (f32[144,6]{0,1:T(8,128)S(1)}, f32[144,6]{0,1:T(8,128)}, u32[]{:S(2)}) copy-start(f32[144,6]{0,1:T(8,128)} %param.8) | copy-start | bytes 10372
  353.2 71.4 %all-to-all-start.1 = ((bf16[8,2,1,72,2048]{4,3,1,2,0:T(8,128)(2,1)}), bf16[8,2,1,72,2048]{4,3,1,2,0:T(8,128)(2,1)}, u32[]{:S(2)}, u32[]{:S(2)}) async-start(bf16[8,2,1,72,2048]{4,3,1,2,0:T(8,128)(2,1)} %fusion.3), calls=%async_computation.1 | async-start | bytes 9437184 | tf_op jit(solution)/shard_map/all_to_all | solution.py:12
  441.5 15.4 %copy-start.1 = (bf16[144,2048]{1,0:T(8,128)(2,1)S(1)}, bf16[144,2048]{1,0:T(8,128)(2,1)}, u32[]{:S(2)}) copy-start(bf16[144,2048]{1,0:T(8,128)(2,1)} %param.6) | copy-start | bytes 1769476
Sparse Core Ops, SparseCore 0:
  9.8 136.4 all-gather.3
  148.8 83.7 all-gather.5
  235.1 83.7 all-gather.7
